TPU v7x, 32 devices: a whole 2x2x4 slice. The times are simulated.
32 devices in a mesh: occ: 8 (over z, x), aux: 4 (over y, core).
Axes of the slice: x: 2, y: 2, z: 4, core: 2. Of those that a mesh axis runs over, the one named last changes fastest.
Arguments:
- half_integrals: bfloat16 [8, 1024, 1024], P(None, 'aux'), may hold values from -1 to 1
- vir_coef: bfloat16 [1024, 768], P(None, 'occ'), may hold values from -0.1875 to 0.1875
- occ_energy: float32 [8], replicated, may hold values from -3 to -0.3
- vir_energy: float32 [768], replicated, may hold values from 0.1 to 2
Outputs:
- three_index: float32 [1024, 8, 768], P('aux', 'occ')
- vir_density: float32 [768, 768], P(('occ', 'aux'))
All inputs are finite; a program needn't handle non-finite values.
Results may differ from a plain program's by a relative error of at most 0.0006.
The roundings to bfloat16 on the way count: a program that leaves them out, or rounds other values in their place, can miss the bound.
Values may be sent and summed in bfloat16 or wider, within the bound.
A program may use at most 64 MiB of HBM per device.

v0:
```python
import jax
import jax.numpy as jnp
from jax import lax
from jax.sharding import PartitionSpec as P


def from_behind(array, axis, by):
    size = lax.axis_size(axis)
    return lax.ppermute(array, axis, [(i, (i + by) % size) for i in range(size)])


def amplitudes(own_block, own_energy, arrival, arrival_energy, vir_energy, slice_energy):
    coulomb = jnp.einsum("jbp,iap->ijba", arrival, own_block, preferred_element_type=jnp.float32)
    denominator = (
        own_energy[:, None, None, None]
        + arrival_energy[None, :, None, None]
        - slice_energy[None, None, :, None]
        - vir_energy[None, None, None, :]
    )
    return (coulomb / denominator).astype(jnp.bfloat16)


def per_device(half_integrals, vir_coef, occ_energy, vir_energy):
    partial_block = jnp.einsum(
        "ipm,ma->iap", half_integrals, vir_coef, preferred_element_type=jnp.float32
    ).astype(jnp.bfloat16)
    local_block = lax.all_to_all(partial_block, "occ", split_axis=0, concat_axis=1, tiled=True)
    own_block = lax.all_gather(local_block, "aux", axis=2, tiled=True)
    cycle_size = lax.axis_size("occ")
    aux_size = lax.axis_size("aux")
    block_rows, virtuals, aux_total = own_block.shape
    slice_width = virtuals // aux_size
    first_virtual = lax.axis_index("aux") * slice_width
    visitor = lax.dynamic_slice_in_dim(own_block, first_virtual, slice_width, 1)
    slice_energy = lax.dynamic_slice_in_dim(vir_energy, first_virtual, slice_width, 0)
    my_index = lax.axis_index("occ")

    def energy_of(anchor):
        return lax.dynamic_slice_in_dim(occ_energy, anchor % cycle_size * block_rows, block_rows, 0)

    own_energy = energy_of(my_index)
    amp_stack = jnp.zeros((cycle_size, block_rows, block_rows, slice_width, virtuals), jnp.bfloat16)
    store_buffer = jnp.zeros((cycle_size, block_rows, slice_width, aux_total), jnp.bfloat16)

    def absorb(ledger, position, arrival, arrival_energy):
        stacked, keeper = ledger
        amplitude = amplitudes(
            own_block, own_energy, arrival, arrival_energy, vir_energy, slice_energy
        )
        stacked = lax.dynamic_update_index_in_dim(stacked, amplitude, position, 0)
        keeper = lax.dynamic_update_index_in_dim(keeper, arrival, position, 0)
        return (stacked, keeper)

    ledger = absorb((amp_stack, store_buffer), 0, visitor, own_energy)

    def one_turn(turn_index, payload):
        ledger, arrival = payload
        arrival = from_behind(arrival, "occ", 1)
        ledger = absorb(ledger, turn_index, arrival, energy_of(my_index - turn_index))
        return (ledger, arrival)

    ledger, arrival = lax.fori_loop(1, cycle_size, one_turn, (ledger, visitor))
    amp_stack, store_buffer = ledger
    three_index = lax.psum_scatter(
        jnp.einsum("sijba,sjbp->pia", amp_stack, store_buffer, preferred_element_type=jnp.float32),
        "aux",
        scatter_dimension=0,
        tiled=True,
    )
    vir_sum = jnp.einsum(
        "sijca,sijcd->ad", amp_stack, amp_stack, preferred_element_type=jnp.float32
    )
    vir_rows = lax.psum_scatter(vir_sum, ("occ", "aux"), scatter_dimension=0, tiled=True)
    return (three_index, vir_rows / (block_rows * cycle_size * virtuals))


def solution(mesh):
    return jax.shard_map(
        per_device,
        mesh=mesh,
        in_specs=(P(None, "aux", None), P(None, "occ"), P(), P()),
        out_specs=(P("aux", "occ", None), P(("occ", "aux"), None)),
        check_vma=False,
    )
```

profile of v0, /device:TPU:0, one launch (start us, length us, event | category | flops | bytes accessed | tf_op | source)
XLA Modules:
  0.0 311.1 jit_solution(6742861085292702216)
XLA Ops:
  7.2 0.0 copy-start
  7.2 0.0 copy-start.4
  7.2 0.0 all-gather.2.cloned.1.call-start
  7.2 0.9 copy-done
  8.1 3.6 %fusion.36 = bf16[8,96,256]{2,1,0:T(8,128)(2,1)S(1)} fusion(bf16[8,256,1024]{2,1,0:T(8,128)(2,1)} %param.6, bf16[1024,96]{0,1:T(8,128)(2,1)S(1)} %copy-done), kind=kOutput, calls=%fused_computation.21 | convolution fusion | flops 402849792 | bytes 4784128 | tf_op jit(solution)/shard_map/ipm,ma->iap/dot_general | solution.py:24
  11.7 19.2 %all_to_all.12 = bf16[8,96,256]{2,1,0:T(8,128)(2,1)} all-to-all(bf16[8,96,256]{2,1,0:T(8,128)(2,1)S(1)} %fusion.36), channel_id=1, replica_groups=mesh['occ'=8,'aux'=4] {'occ'}, dimensions={0} | all-to-all | bytes 786432 | tf_op jit(solution)/shard_map/all_to_all | solution.py:27
  30.9 0.0 all-gather.2.cloned.1.call-update
  31.0 0.0 reduce-scatter.5.cloned.1.call-start
  31.0 0.6 dynamic_slice.23
  32.7 0.0 copy-done.3
  32.7 0.1 broadcast_subtract_fusion.1
  32.8 16.9 %all-gather.2.cloned.1.call-done = bf16[1,768,1024]{2,1,0:T(8,128)(2,1)} async-done(((bf16[1,768,256]{2,1,0:T(8,128)(2,1)}), bf16[1,768,1024]{2,1,0:T(8,128)(2,1)}) %all-gather.2.cloned.1.call-update) | async-done | bytes 1572880 | tf_op jit(solution)/shard_map/all_gather | solution.py:28
  49.6 1.0 constant_dynamic-slice_fusion
  50.7 2.1 fusion.43
  52.8 0.2 dynamic_update_slice.34
  52.9 1.0 fusion.49
  54.0 2.0 dynamic_update_slice.35
  56.0 102.9 %while.21 = (s32[]{:T(128)}, bf16[8,1,1,192,768]{4,3,2,1,0:T(8,128)(2,1)S(1)}, bf16[8,1,192,1024]{3,2,1,0:T(8,128)(2,1)}, bf16[1,192,1024]{2,1,0:T(8,128)(2,1)S(...) while((s32[]{:T(128)}, ...), condition=%wide.region_1.2_spmd, body=%wide.region_0.1_spmd.sunk | while | flops 302432480 | bytes 5413790 | solution.py:62
  56.0 1.5 collective-permute-start
  57.4 0.7 dynamic_slice.30
  59.4 10.6 %collective-permute-done = bf16[1,192,1024]{2,1,0:T(8,128)(2,1)S(1)} collective-permute-done((bf16[1,192,1024]{2,1,0:T(8,128)(2,1)S(1)}, bf16[1,192,1024]{2,1,0:T(8,128)(2,1)S(1)}, u32[]{:S(2)}, u32[]{:S(2)}) %collective-permute-start) | collective-permute-done | bytes 393248 | tf_op jit(solution)/shard_map/while/body/eval_jaxpr/ppermute | solution.py:9
  70.0 0.8 bitcast_dynamic-update-slice_fusion.2
  70.7 2.1 fusion.55
  72.8 0.1 collective-permute-start
  72.9 0.7 dynamic_slice.30
  74.9 11.2 %collective-permute-done = bf16[1,192,1024]{2,1,0:T(8,128)(2,1)S(1)} collective-permute-done((bf16[1,192,1024]{2,1,0:T(8,128)(2,1)S(1)}, bf16[1,192,1024]{2,1,0:T(8,128)(2,1)S(1)}, u32[]{:S(2)}, u32[]{:S(2)}) %collective-permute-start) | collective-permute-done | bytes 393248 | tf_op jit(solution)/shard_map/while/body/eval_jaxpr/ppermute | solution.py:9
  86.0 0.8 bitcast_dynamic-update-slice_fusion.2
  86.8 2.1 fusion.55
  88.9 0.1 collective-permute-start
  89.0 0.7 dynamic_slice.30
  90.9 10.3 %collective-permute-done = bf16[1,192,1024]{2,1,0:T(8,128)(2,1)S(1)} collective-permute-done((bf16[1,192,1024]{2,1,0:T(8,128)(2,1)S(1)}, bf16[1,192,1024]{2,1,0:T(8,128)(2,1)S(1)}, u32[]{:S(2)}, u32[]{:S(2)}) %collective-permute-start) | collective-permute-done | bytes 393248 | tf_op jit(solution)/shard_map/while/body/eval_jaxpr/ppermute | solution.py:9
  101.3 0.8 bitcast_dynamic-update-slice_fusion.2
  102.1 2.1 fusion.55
  104.2 0.1 collective-permute-start
  104.3 0.7 dynamic_slice.30
  106.2 9.4 %collective-permute-done = bf16[1,192,1024]{2,1,0:T(8,128)(2,1)S(1)} collective-permute-done((bf16[1,192,1024]{2,1,0:T(8,128)(2,1)S(1)}, bf16[1,192,1024]{2,1,0:T(8,128)(2,1)S(1)}, u32[]{:S(2)}, u32[]{:S(2)}) %collective-permute-start) | collective-permute-done | bytes 393248 | tf_op jit(solution)/shard_map/while/body/eval_jaxpr/ppermute | solution.py:9
  115.6 0.8 bitcast_dynamic-update-slice_fusion.2
  116.4 2.1 fusion.55
  118.5 0.1 collective-permute-start
  118.6 0.7 dynamic_slice.30
  120.5 8.6 %collective-permute-done = bf16[1,192,1024]{2,1,0:T(8,128)(2,1)S(1)} collective-permute-done((bf16[1,192,1024]{2,1,0:T(8,128)(2,1)S(1)}, bf16[1,192,1024]{2,1,0:T(8,128)(2,1)S(1)}, u32[]{:S(2)}, u32[]{:S(2)}) %collective-permute-start) | collective-permute-done | bytes 393248 | tf_op jit(solution)/shard_map/while/body/eval_jaxpr/ppermute | solution.py:9
  129.1 0.8 bitcast_dynamic-update-slice_fusion.2
  129.9 2.1 fusion.55
  132.0 0.1 collective-permute-start
  132.1 0.7 dynamic_slice.30
  134.0 8.5 %collective-permute-done = bf16[1,192,1024]{2,1,0:T(8,128)(2,1)S(1)} collective-permute-done((bf16[1,192,1024]{2,1,0:T(8,128)(2,1)S(1)}, bf16[1,192,1024]{2,1,0:T(8,128)(2,1)S(1)}, u32[]{:S(2)}, u32[]{:S(2)}) %collective-permute-start) | collective-permute-done | bytes 393248 | tf_op jit(solution)/shard_map/while/body/eval_jaxpr/ppermute | solution.py:9
  142.6 0.8 bitcast_dynamic-update-slice_fusion.2
  143.3 2.1 fusion.55
  145.4 0.1 collective-permute-start
  145.5 0.7 dynamic_slice.30
  147.5 8.5 %collective-permute-done = bf16[1,192,1024]{2,1,0:T(8,128)(2,1)S(1)} collective-permute-done((bf16[1,192,1024]{2,1,0:T(8,128)(2,1)S(1)}, bf16[1,192,1024]{2,1,0:T(8,128)(2,1)S(1)}, u32[]{:S(2)}, u32[]{:S(2)}) %collective-permute-start) | collective-permute-done | bytes 393248 | tf_op jit(solution)/shard_map/while/body/eval_jaxpr/ppermute | solution.py:9
  156.0 0.8 bitcast_dynamic-update-slice_fusion.2
  156.8 2.1 fusion.55
  158.9 1.4 copy-done.2
  160.3 6.1 %fusion.28 = f32[768,768]{1,0:T(8,128)} fusion(bf16[8,1,1,192,768]{4,3,2,1,0:T(8,128)(2,1)} %copy-done.2), kind=kOutput, calls=%fused_computation.16 | convolution fusion | flops 1811939328 | bytes 4718592 | tf_op jit(solution)/shard_map/sijca,sijcd->ad/dot_general | solution.py:70
  166.3 0.0 reduce-scatter.5.cloned.1.call-update
  166.4 0.0 reduce-scatter.3.cloned.1.call-start
  166.4 0.0 copy-done.1
  166.4 6.0 %fusion.23 = f32[1024,1,768]{2,0,1:T(8,128)} fusion(bf16[8,1,1,192,768]{4,3,2,1,0:T(8,128)(2,1)} %copy-done.2, bf16[8,1,192,1024]{3,2,1,0:T(8,128)(2,1)S(1)} %copy-done.1), kind=kOutput, calls=%fused_computation.15 | convolution fusion | flops 2415919104 | bytes 8650752 | tf_op jit(solution)/shard_map/sijba,sjbp->pia/dot_general | solution.py:65
  172.4 0.0 reduce-scatter.3.cloned.1.call-update
  172.4 89.9 %reduce-scatter.5.cloned.1.call-done = f32[24,768]{1,0:T(8,128)} async-done(((f32[768,768]{1,0:T(8,128)}), f32[24,768]{1,0:T(8,128)}) %reduce-scatter.5.cloned.1.call-update) | async-done | bytes 73744 | tf_op jit(solution)/shard_map/reduce_scatter | solution.py:73
  262.3 1.5 broadcast_multiply_fusion
  263.9 37.9 %reduce-scatter.3.cloned.1.call-done = f32[256,1,768]{2,0,1:T(8,128)} async-done(((f32[1024,1,768]{2,0,1:T(8,128)}), f32[256,1,768]{2,0,1:T(8,128)}) %reduce-scatter.3.cloned.1.call-update) | async-done | bytes 786448 | tf_op jit(solution)/shard_map/reduce_scatter | solution.py:64
  301.7 2.8 copy.6
  (18 shorter events, 0.2 us)
Async XLA Ops:
  7.2 0.9 copy-start
  7.2 23.9 %copy-start.4 = (f32[8]{0:T(128)S(1)}, f32[8]{0:T(128)}, u32[]{:S(2)}) copy-start(f32[8]{0:T(128)} %param.8) | copy-start | bytes 100
  7.2 25.5 %copy-start.3 = (f32[768]{0:T(1024)S(1)}, f32[768]{0:T(1024)}, u32[]{:S(2)}) copy-start(f32[768]{0:T(1024)} %param.9) | copy-start | bytes 9220
  7.2 42.4 %all-gather.2.cloned.1.call-start = ((), (), s32[]{:S(2)}) async-start(), calls=%async_computation.3 | async-start | bytes 1966080 | tf_op jit(solution)/shard_map/all_gather | solution.py:28
  31.0 231.4 %reduce-scatter.5.cloned.1.call-start = ((), (), s32[]{:S(2)}) async-start(), calls=%async_computation.5 | async-start | bytes 2433024 | tf_op jit(solution)/shard_map/reduce_scatter | solution.py:73
  56.0 14.0 %collective-permute-start = (bf16[1,192,1024]{2,1,0:T(8,128)(2,1)S(1)}, bf16[1,192,1024]{2,1,0:T(8,128)(2,1)S(1)}, u32[]{:S(2)}, u32[]{:S(2)}) collective-permute-start(bf16[1,192,1024]{2,1,0:T(8,128)(2,1)S(1)} %get-tuple-element.424), channel_id=1, source_target_pairs={{0,4},{4,8},{8,12},{12,16},{16,20},{20,24},{24,28},{28,0},{1,5},{5... | collective-permute-start | bytes 1179656 | tf_op jit(solution)/shard_map/while/body/eval_jaxpr/ppermute | solution.py:9
  72.8 13.2 %collective-permute-start = (bf16[1,192,1024]{2,1,0:T(8,128)(2,1)S(1)}, bf16[1,192,1024]{2,1,0:T(8,128)(2,1)S(1)}, u32[]{:S(2)}, u32[]{:S(2)}) collective-permute-start(bf16[1,192,1024]{2,1,0:T(8,128)(2,1)S(1)} %get-tuple-element.424), channel_id=1, source_target_pairs={{0,4},{4,8},{8,12},{12,16},{16,20},{20,24},{24,28},{28,0},{1,5},{5... | collective-permute-start | bytes 1179656 | tf_op jit(solution)/shard_map/while/body/eval_jaxpr/ppermute | solution.py:9
  88.9 12.3 %collective-permute-start = (bf16[1,192,1024]{2,1,0:T(8,128)(2,1)S(1)}, bf16[1,192,1024]{2,1,0:T(8,128)(2,1)S(1)}, u32[]{:S(2)}, u32[]{:S(2)}) collective-permute-start(bf16[1,192,1024]{2,1,0:T(8,128)(2,1)S(1)} %get-tuple-element.424), channel_id=1, source_target_pairs={{0,4},{4,8},{8,12},{12,16},{16,20},{20,24},{24,28},{28,0},{1,5},{5... | collective-permute-start | bytes 1179656 | tf_op jit(solution)/shard_map/while/body/eval_jaxpr/ppermute | solution.py:9
  104.2 11.4 %collective-permute-start = (bf16[1,192,1024]{2,1,0:T(8,128)(2,1)S(1)}, bf16[1,192,1024]{2,1,0:T(8,128)(2,1)S(1)}, u32[]{:S(2)}, u32[]{:S(2)}) collective-permute-start(bf16[1,192,1024]{2,1,0:T(8,128)(2,1)S(1)} %get-tuple-element.424), channel_id=1, source_target_pairs={{0,4},{4,8},{8,12},{12,16},{16,20},{20,24},{24,28},{28,0},{1,5},{5... | collective-permute-start | bytes 1179656 | tf_op jit(solution)/shard_map/while/body/eval_jaxpr/ppermute | solution.py:9
  118.5 10.6 %collective-permute-start = (bf16[1,192,1024]{2,1,0:T(8,128)(2,1)S(1)}, bf16[1,192,1024]{2,1,0:T(8,128)(2,1)S(1)}, u32[]{:S(2)}, u32[]{:S(2)}) collective-permute-start(bf16[1,192,1024]{2,1,0:T(8,128)(2,1)S(1)} %get-tuple-element.424), channel_id=1, source_target_pairs={{0,4},{4,8},{8,12},{12,16},{16,20},{20,24},{24,28},{28,0},{1,5},{5... | collective-permute-start | bytes 1179656 | tf_op jit(solution)/shard_map/while/body/eval_jaxpr/ppermute | solution.py:9
  132.0 10.5 %collective-permute-start = (bf16[1,192,1024]{2,1,0:T(8,128)(2,1)S(1)}, bf16[1,192,1024]{2,1,0:T(8,128)(2,1)S(1)}, u32[]{:S(2)}, u32[]{:S(2)}) collective-permute-start(bf16[1,192,1024]{2,1,0:T(8,128)(2,1)S(1)} %get-tuple-element.424), channel_id=1, source_target_pairs={{0,4},{4,8},{8,12},{12,16},{16,20},{20,24},{24,28},{28,0},{1,5},{5... | collective-permute-start | bytes 1179656 | tf_op jit(solution)/shard_map/while/body/eval_jaxpr/ppermute | solution.py:9
  145.4 10.5 %collective-permute-start = (bf16[1,192,1024]{2,1,0:T(8,128)(2,1)S(1)}, bf16[1,192,1024]{2,1,0:T(8,128)(2,1)S(1)}, u32[]{:S(2)}, u32[]{:S(2)}) collective-permute-start(bf16[1,192,1024]{2,1,0:T(8,128)(2,1)S(1)} %get-tuple-element.424), channel_id=1, source_target_pairs={{0,4},{4,8},{8,12},{12,16},{16,20},{20,24},{24,28},{28,0},{1,5},{5... | collective-permute-start | bytes 1179656 | tf_op jit(solution)/shard_map/while/body/eval_jaxpr/ppermute | solution.py:9
  158.9 1.4 copy-start.2
  160.3 6.1 %copy-start.1 = (bf16[8,1,192,1024]{3,2,1,0:T(8,128)(2,1)S(1)}, bf16[8,1,192,1024]{3,2,1,0:T(8,128)(2,1)}, u32[]{:S(2)}) copy-start(bf16[8,1,192,1024]{3,2,1,0:T(8,128)(2,1)} %get-tuple-element.319) | copy-start | bytes 9437188
  166.4 135.4 %reduce-scatter.3.cloned.1.call-start = ((), (), s32[]{:S(2)}) async-start(), calls=%async_computation.4 | async-start | bytes 3932160 | tf_op jit(solution)/shard_map/reduce_scatter | solution.py:64
Sparse Core Ops, SparseCore 0:
  31.1 18.5 all-gather.1
  166.5 95.8 reduce-scatter.4
  264.9 36.8 reduce-scatter.2
where the time goes:
time: 312 us; the launch traced here: 311 us
  waiting for transfers between devices  212 us (68%)
  matrix products  32.3 us (10%)
  local copies, waits for them, and re-layouts  20.2 us (6%)
  blocking collectives  19.2 us (6%)
  between operations  15 us (5%)
  loops' own time  9.07 us (3%)
    reduce_scatter x1, waiting for transfers between devices, per_device(): lax.psum_scatter(vir_sum, ('occ', 'aux'), scatter_dimension=0, tiled=True)  89.9 us
    ppermute x7, waiting for transfers between devices, from_behind(): lax.ppermute(array, axis, [(i, (i + by) % size) for i in range(size)])  67.1 us
    reduce_scatter x1, waiting for transfers between devices, per_device(): lax.psum_scatter(jnp.einsum('sijba,sjbp->pia', amp_stack, store_buffer, p...  37.9 us
    all_to_all x1, blocking collectives, per_device(): lax.all_to_all(partial_block, 'occ', split_axis=0, concat_axis=1, tiled=T...  19.2 us
    all_gather x1, waiting for transfers between devices, per_device(): own_block = lax.all_gather(local_block, 'aux', axis=2, tiled=True)  16.9 us
    dot_general x8, matrix products, amplitudes(): jnp.einsum('jbp,iap->ijba', arrival, own_block, preferred_element_type=jn...  16.7 us
    another operation x1, loops' own time, per_device(): ledger, arrival = lax.fori_loop(1, cycle_size, one_turn, (ledger, visitor))  9.07 us
    dynamic_update_slice x8, local copies, waits for them, and re-layouts, absorb(): keeper = lax.dynamic_update_index_in_dim(keeper, arrival, position, 0)  7.49 us
  transfers between devices with their start and end apart: 10, of which 10 were waited for; matrix products, arithmetic and copies ran while one was open for 4% of the time, Pallas kernels for 0%

commit v1 on v0

v1 whole, which is shorter than its diff:
```python
import functools

import jax
import jax.numpy as jnp
from jax import lax
from jax.experimental import pallas as pl
from jax.experimental.pallas import tpu as pltpu
from jax.sharding import PartitionSpec as P

MESH = pl.DeviceIdType.MESH
F32 = jnp.float32
LIMIT = 56 * 1024 * 1024


def remote(src, dst, send, recv, target):
    return pltpu.make_async_remote_copy(
        src_ref=src, dst_ref=dst, send_sem=send, recv_sem=recv, device_id=target, device_id_type=MESH
    )


def nearest_first(z, k, count):
    near = jnp.minimum(z, count - 1 - z)
    step = (k + 1) // 2
    both = z + step * (2 * (k % 2) - 1)
    low = z < count - 1 - z
    return jnp.where(k <= 2 * near, both, jnp.where(low, k, count - 1 - k))


def amplitude_kernel(n, aux, occ_e, own, row_e, col_e, three, vir, held, amps, sem_recv, sem_up, sem_down, sem_side, sem_own):
    o = lax.axis_index("occ")
    s = lax.axis_index("aux")
    z, low = o // 2, o % 2
    nz = n // 2
    virtuals, total = own.shape
    width = virtuals // aux
    above, below, side = o + 2, o - 2, 2 * z + 1 - low

    barrier = pltpu.get_barrier_semaphore()
    for peer in ((o + 2) % n, (o + n - 2) % n, side):
        pl.semaphore_signal(barrier, inc=1, device_id=(peer, s), device_id_type=MESH)

    def slot(index):
        return held.at[pl.ds(pl.multiple_of(index * width, width), width)]

    mine = own.at[pl.ds(pl.multiple_of(s * width, width), width)]
    local = pltpu.make_async_copy(mine, slot(o), sem_own)
    local.start()
    three[...] = jnp.zeros_like(three)
    vir[...] = jnp.zeros_like(vir)
    pl.semaphore_wait(barrier, 3)

    def sends(chain, src):
        block = 2 * chain + low
        up = remote(src, slot(block), sem_up.at[chain], sem_recv.at[block], (above, s))
        down = remote(src, slot(block), sem_down.at[chain], sem_recv.at[block], (below, s))
        across = remote(src, slot(block), sem_side.at[chain], sem_recv.at[block], (side, s))
        return (
            (jnp.logical_and(chain <= z, z < nz - 1), up),
            (jnp.logical_and(chain >= z, z > 0), down),
            (chain >= 0, across),
        )

    def each_send(chain, src, act):
        for allowed, copy in sends(chain, src):
            pl.when(allowed)(functools.partial(act, copy))

    each_send(z, mine, lambda copy: copy.start())

    def arrived(block):
        remote(slot(block), slot(block), sem_side.at[0], sem_recv.at[block], (side, s)).wait_recv()

    def absorb(block):
        rows = pl.ds(pl.multiple_of(block * width, width), width)
        coulomb = lax.dot_general(
            held[rows, :], own[...], (((1,), (1,)), ((), ())), preferred_element_type=F32
        )
        denominator = occ_e[o] + occ_e[block] - col_e[...] - row_e[...]
        amps[rows, :] = (coulomb / denominator).astype(jnp.bfloat16)

    def pair(chain):
        absorb(2 * chain + low)
        arrived(2 * chain + 1 - low)
        absorb(2 * chain + 1 - low)
        rows = pl.ds(pl.multiple_of(chain * 2 * width, 2 * width), 2 * width)
        contract = (((0,), (0,)), ((), ()))

        @pl.loop(0, virtuals // 256)
        def _(t):
            cols = pl.ds(pl.multiple_of(t * 256, 256), 256)
            vir[cols, :] += lax.dot_general(amps[rows, cols], amps[rows, :], contract, preferred_element_type=F32)

        @pl.loop(0, total // 256)
        def _(t):
            cols = pl.ds(pl.multiple_of(t * 256, 256), 256)
            three[cols, :] += lax.dot_general(held[rows, cols], amps[rows, :], contract, preferred_element_type=F32)

    local.wait()

    @pl.loop(1, nz)
    def _(k):
        chain = nearest_first(z, k, nz)
        arrived(2 * chain + low)
        each_send(chain, slot(2 * chain + low), lambda copy: copy.start())
        pair(nearest_first(z, k - 1, nz))

    pair(nearest_first(z, nz - 1, nz))

    @pl.loop(0, nz)
    def _(chain):
        each_send(chain, slot(2 * chain + low), lambda copy: copy.wait_send())


def reduce_kernel(
    n, nq, scale, three, vir, three_out, vir_out,
    t_pair, t_out, t_far, v_pair, v_sum, v_side, v_line, v_chain, v_col, v_far,
    pair_send, pair_recv, t_send, t_recv, vp_send, vp_recv, x_send, x_recv, z_send, z_recv, y_send, y_recv,
):
    o = lax.axis_index("occ")
    s = lax.axis_index("aux")
    q, c = s // 2, s % 2
    z, low = o // 2, o % 2
    nz = n // 2
    partner = (o, 2 * q + 1 - c)
    side = (2 * z + 1 - low, s)

    barrier = pltpu.get_barrier_semaphore()
    pl.semaphore_signal(barrier, inc=1, device_id=partner, device_id_type=MESH)
    pl.semaphore_signal(barrier, inc=1, device_id=side, device_id_type=MESH)
    for d in range(1, nq):
        pl.semaphore_signal(barrier, inc=1, device_id=(o, 2 * ((q + d) % nq) + c), device_id_type=MESH)
    for d in range(1, nz):
        pl.semaphore_signal(barrier, inc=1, device_id=(2 * ((z + d) % nz) + low, s), device_id_type=MESH)
    pl.semaphore_wait(barrier, nq + nz)

    v_swap = remote(vir.at[:, :, 1 - c], v_pair, vp_send, vp_recv, partner)
    v_swap.start()

    def swap(d):
        there = (q + d) % nq
        return remote(three.at[there, 1 - c], t_pair.at[d], pair_send.at[d], pair_recv.at[d], partner)

    def spread(d):
        return remote(t_out.at[d], t_far.at[d], t_send.at[d], t_recv.at[d], (o, 2 * ((q + d) % nq) + c))

    order = list(range(1, nq)) + [0]
    for d in order:
        swap(d).start()
    v_swap.wait()
    v_sum[...] = (vir[:, :, c] + v_pair[...]).reshape(v_sum.shape)
    x_swap = remote(v_sum.at[:, 1 - low], v_side, x_send, x_recv, side)
    x_swap.start()
    for d in order[:-1]:
        swap(d).wait()
        t_out[d] = three[(q + d) % nq, c] + t_pair[d]
        spread(d).start()
    swap(0).wait()
    three_out[...] = three[q, c] + t_pair[0]

    x_swap.wait()
    v_line[...] = v_sum[:, low] + v_side[...]

    def along(d):
        there = (z + d) % nz
        return remote(v_line.at[there], v_chain.at[d], z_send.at[d], z_recv.at[d], (2 * there + low, s))

    for d in range(1, nz):
        along(d).start()
    v_col[...] = v_line[z]
    for d in range(1, nz):
        along(d).wait()
        v_col[...] += v_chain[d]

    def between(d):
        there = (q + d) % nq
        return remote(v_col.at[there], v_far.at[d], y_send.at[d], y_recv.at[d], (o, 2 * there + c))

    for d in range(1, nq):
        between(d).start()
    for d in order[:-1]:
        spread(d).wait()
        three_out[...] += t_far[d]
    rows = v_col[q]
    for d in range(1, nq):
        between(d).wait()
        rows += v_far[d]
    vir_out[...] = rows / scale


def per_device(half_integrals, vir_coef, occ_energy, vir_energy):
    partial_block = jnp.einsum(
        "ipm,ma->iap", half_integrals, vir_coef, preferred_element_type=F32
    ).astype(jnp.bfloat16)
    local_block = lax.all_to_all(partial_block, "occ", split_axis=0, concat_axis=1, tiled=True)
    own = lax.all_gather(local_block, "aux", axis=2, tiled=True)[0]
    n, aux = lax.axis_size("occ"), lax.axis_size("aux")
    nz, nq = n // 2, aux // 2
    virtuals, total = own.shape
    width, tile, rows = virtuals // aux, total // aux, virtuals // (n * aux)
    row_e = vir_energy[None, :]
    col_e = lax.dynamic_slice_in_dim(vir_energy, lax.axis_index("aux") * width, width, 0)[:, None]
    vmem = pl.BlockSpec(memory_space=pltpu.VMEM)
    dma = pltpu.SemaphoreType.DMA
    three, vir = pl.pallas_call(
        functools.partial(amplitude_kernel, n, aux),
        out_shape=(
            jax.ShapeDtypeStruct((total, virtuals), F32),
            jax.ShapeDtypeStruct((virtuals, virtuals), F32),
        ),
        in_specs=[pl.BlockSpec(memory_space=pltpu.SMEM), vmem, vmem, vmem],
        out_specs=(vmem, vmem),
        scratch_shapes=[
            pltpu.VMEM((n * width, total), jnp.bfloat16),
            pltpu.VMEM((n * width, virtuals), jnp.bfloat16),
            dma((n,)), dma((nz,)), dma((nz,)), dma((nz,)), dma,
        ],
        compiler_params=pltpu.CompilerParams(
            collective_id=0, has_side_effects=True, vmem_limit_bytes=LIMIT
        ),
        name="amplitude",
    )(occ_energy, own, row_e, col_e)

    def room(*shape):
        return pltpu.VMEM(shape, F32)

    three_index, vir_rows = pl.pallas_call(
        functools.partial(reduce_kernel, n, nq, float(n * virtuals)),
        out_shape=(
            jax.ShapeDtypeStruct((tile, virtuals), F32),
            jax.ShapeDtypeStruct((rows, virtuals), F32),
        ),
        in_specs=[vmem, vmem],
        out_specs=(vmem, vmem),
        scratch_shapes=[
            room(nq, tile, virtuals), room(nq, tile, virtuals), room(nq, tile, virtuals),
            room(n, nq, rows, virtuals), room(nz, 2, nq, rows, virtuals),
            room(nz, nq, rows, virtuals), room(nz, nq, rows, virtuals), room(nz, nq, rows, virtuals),
            room(nq, rows, virtuals), room(nq, rows, virtuals),
            dma((nq,)), dma((nq,)), dma((nq,)), dma((nq,)), dma, dma, dma, dma,
            dma((nz,)), dma((nz,)), dma((nq,)), dma((nq,)),
        ],
        compiler_params=pltpu.CompilerParams(
            collective_id=1, has_side_effects=True, vmem_limit_bytes=LIMIT
        ),
        name="reduce",
    )(
        three.reshape(nq, 2, tile, virtuals),
        vir.reshape(n, nq, 2, rows, virtuals),
    )
    return three_index[:, None, :], vir_rows


def solution(mesh):
    return jax.shard_map(
        per_device,
        mesh=mesh,
        in_specs=(P(None, "aux", None), P(None, "occ"), P(), P()),
        out_specs=(P("aux", "occ", None), P(("occ", "aux"), None)),
        check_vma=False,
    )
```

time: 312 us -> 151 us (0.48)
  waiting for transfers between devices: 212 us -> 17.3 us
  Pallas kernels: 0 us -> 90.3 us
  matrix products: 32.3 us -> 3.6 us
  local copies, waits for them, and re-layouts: 20.2 us -> 6.64 us
  loops' own time: 9.07 us -> 0 us
    reduce_scatter x2 -> x0, waiting for transfers between devices: 128 us -> none  [the longest x1 89.9 us: per_device(): lax.psum_scatter(vir_sum, ('occ', 'aux'), scatter_dimension=0, tiled=True)]
    pallas_call x0 -> x2, Pallas kernels: none -> 90.3 us  [the longest x1 50.2 us: per_device(): pl.pallas_call(functools.partial(amplitude_kernel, n, aux), out_shape=(ja...]
    ppermute x7 -> x0, waiting for transfers between devices: 67.1 us -> none  [from_behind(): lax.ppermute(array, axis, [(i, (i + by) % size) for i in range(size)])]
    dot_general x10 -> x0, matrix products: 28.7 us -> none  [the longest x8 16.7 us: amplitudes(): jnp.einsum('jbp,iap->ijba', arrival, own_block, preferred_element_type=jn...]
    another operation x1 -> x0, loops' own time: 9.07 us -> none  [per_device(): ledger, arrival = lax.fori_loop(1, cycle_size, one_turn, (ledger, visitor))]
    dynamic_update_slice x9 -> x0, local copies, waits for them, and re-layouts: 7.65 us -> none  [the longest x8 7.49 us: absorb(): keeper = lax.dynamic_update_index_in_dim(keeper, arrival, position, 0)]
    dynamic_slice x9 -> x1, local copies, waits for them, and re-layouts: 6.25 us -> 0.07 us  [per_device(): lax.dynamic_slice_in_dim(vir_energy, lax.axis_index('aux') * width, width...]
  transfers between devices with their start and end apart: 10 -> 1, of which waited for: 10 -> 1; matrix products, arithmetic and copies ran while one was open for 4% -> 1% of each run, Pallas kernels for 0% -> 0%
where the time goes in v1:
time: 151 us
  Pallas kernels  90.3 us (60%)
  blocking collectives  19.2 us (13%)
  waiting for transfers between devices  17.3 us (11%)
  between operations  14.1 us (9%)
  local copies, waits for them, and re-layouts  6.64 us (4%)
  matrix products  3.6 us (2%)
    pallas_call x1, Pallas kernels, per_device(): pl.pallas_call(functools.partial(amplitude_kernel, n, aux), out_shape=(ja...  50.2 us
    pallas_call x1, Pallas kernels, per_device(): pl.pallas_call(functools.partial(reduce_kernel, n, nq, float(n * virtuals...  40.2 us
    all_to_all x1, blocking collectives, per_device(): lax.all_to_all(partial_block, 'occ', split_axis=0, concat_axis=1, tiled=T...  19.2 us
    all_gather x1, waiting for transfers between devices, per_device(): own = lax.all_gather(local_block, 'aux', axis=2, tiled=True)[0]  17.2 us
    unnamed x6, local copies, waits for them, and re-layouts  5.22 us
    dot_general x1, matrix products, per_device(): jnp.einsum('ipm,ma->iap', half_integrals, vir_coef, preferred_element_typ...  3.6 us
  transfers between devices with their start and end apart: 1, of which 1 were waited for; matrix products, arithmetic and copies ran while one was open for 1% of the time, Pallas kernels for 0%

profile of v1, /device:TPU:0, one launch (start us, length us, event | category | flops | bytes accessed | tf_op | source)
XLA Modules:
  0.0 151.2 jit_solution(689851114128605486)
XLA Ops:
  7.2 0.0 copy-start
  7.2 0.0 copy-start.1
  7.2 0.0 all-gather.2.cloned.1.call-start
  7.2 0.9 copy-done
  8.1 3.6 %fusion = bf16[8,96,256]{2,1,0:T(8,128)(2,1)S(1)} fusion(bf16[8,256,1024]{2,1,0:T(8,128)(2,1)} %param.4, bf16[1024,96]{0,1:T(8,128)(2,1)S(1)} %copy-done), kind=kOutput, calls=%fused_computation.1 | convolution fusion | flops 402849792 | bytes 4784128 | tf_op jit(solution)/shard_map/ipm,ma->iap/dot_general | solution.py:190
  11.7 19.2 %all_to_all.12 = bf16[8,96,256]{2,1,0:T(8,128)(2,1)} all-to-all(bf16[8,96,256]{2,1,0:T(8,128)(2,1)S(1)} %fusion), channel_id=1, replica_groups=mesh['occ'=8,'aux'=4] {'occ'}, dimensions={0} | all-to-all | bytes 786432 | tf_op jit(solution)/shard_map/all_to_all | solution.py:193
  30.9 0.0 all-gather.2.cloned.1.call-update
  31.0 0.0 copy-done.1
  31.0 0.6 broadcast_in_dim.9.row_e
  31.6 0.1 dynamic_slice.3
  31.6 0.8 copy.7.col_e
  32.4 17.2 %all-gather.2.cloned.1.call-done = bf16[1,768,1024]{2,1,0:T(8,128)(2,1)} async-done(((bf16[1,768,256]{2,1,0:T(8,128)(2,1)}), bf16[1,768,1024]{2,1,0:T(8,128)(2,1)}) %all-gather.2.cloned.1.call-update) | async-done | bytes 1572880 | tf_op jit(solution)/shard_map/all_gather | solution.py:194
  49.6 50.2 %amplitude.1 = (f32[1024,768]{1,0:T(8,128)}, f32[768,768]{1,0:T(8,128)}) custom-call(f32[8]{0:T(128)} %occ_e.1, bf16[768,1024]{1,0:T(8,128)(2,1)} %bitcast.15, f32[1,768]{1,0:T(1,128)} %broadcast_in_dim.9.row_e, f32[192,1]{1,0:T(8,128)} %copy.7.col_e), custom_call_target="tpu_custom_call" | custom-call | tf_op jit(solution)/shard_map/amplitude/pallas_call | solution.py:203
  99.8 40.2 %reduce.1 = (f32[256,768]{1,0:T(8,128)}, f32[24,768]{1,0:T(8,128)}) custom-call(f32[2,2,256,768]{3,2,1,0:T(8,128)} %bitcast.12, f32[8,2,2,24,768]{4,3,2,1,0:T(8,128)} %bitcast.13), custom_call_target="tpu_custom_call" | custom-call | tf_op jit(solution)/shard_map/reduce/pallas_call | solution.py:225
  140.0 2.8 %copy.8 = f32[256,1,768]{2,1,0:T(1,128)} copy(f32[256,1,768]{2,0,1:T(8,128)} %bitcast.16) | data formatting | bytes 1572864
  142.8 1.5 %copy.10 = f32[24,768]{1,0:T(8,128)} copy(f32[24,768]{1,0:T(8,128)} %get-tuple-element.17) | data formatting | bytes 147456
Async XLA Ops:
  7.2 0.9 copy-start
  7.2 23.8 %copy-start.1 = (f32[768]{0:T(1024)S(1)}, f32[768]{0:T(1024)}, u32[]{:S(2)}) copy-start(f32[768]{0:T(1024)} %param.7) | copy-start | bytes 9220
  7.2 42.4 %all-gather.2.cloned.1.call-start = ((), (), s32[]{:S(2)}) async-start(), calls=%async_computation.1 | async-start | bytes 1966080 | tf_op jit(solution)/shard_map/all_gather | solution.py:194
Sparse Core Ops, SparseCore 0:
  31.1 18.5 all-gather.1

commit v2 on v1

v2 whole, which is shorter than its diff:
```python
import functools

import jax
import jax.numpy as jnp
from jax import lax
from jax.experimental import pallas as pl
from jax.experimental.pallas import tpu as pltpu
from jax.sharding import PartitionSpec as P

MESH = pl.DeviceIdType.MESH
F32 = jnp.float32
LIMIT = 56 * 1024 * 1024


def remote(src, dst, send, recv, target):
    return pltpu.make_async_remote_copy(
        src_ref=src, dst_ref=dst, send_sem=send, recv_sem=recv, device_id=target, device_id_type=MESH
    )


def nearest_first(z, k, count):
    near = jnp.minimum(z, count - 1 - z)
    step = (k + 1) // 2
    both = z + step * (2 * (k % 2) - 1)
    low = z < count - 1 - z
    return jnp.where(k <= 2 * near, both, jnp.where(low, k, count - 1 - k))


def amplitude_kernel(
    n, nq, occ_e, half, coef, row_e, col_e, three, vir,
    ints, full, own, held, gift, amps,
    i_sem, c_copy, o_copy, c_recv, c_up, c_down, c_side, cp_send, cp_recv,
    own_send, own_recv, fw_send, fw_recv, pr_send, pr_recv, g_send, g_recv,
    h_recv, h_up, h_down, h_side,
):
    o = lax.axis_index("occ")
    s = lax.axis_index("aux")
    q, c = s // 2, s % 2
    z, low = o // 2, o % 2
    nz = n // 2
    width = amps.shape[0] // n
    part = coef.shape[1]
    cut = coef.shape[2]
    virtuals = amps.shape[1]
    above, below, side = o + 2, o - 2, 2 * z + 1 - low
    partner = (o, 2 * q + 1 - c)

    barrier = pltpu.get_barrier_semaphore()
    for peer in ((o + 2) % n, (o + n - 2) % n, side):
        pl.semaphore_signal(barrier, inc=1, device_id=(peer, s), device_id_type=MESH)
    pl.semaphore_signal(barrier, inc=1, device_id=partner, device_id_type=MESH)
    for d in range(1, nq):
        pl.semaphore_signal(barrier, inc=1, device_id=(o, 2 * ((q + d) % nq) + c), device_id_type=MESH)

    fetch = pltpu.make_async_copy(half, ints, i_sem)
    fetch.start()

    def span(index, size):
        return pl.ds(pl.multiple_of(index * size, size), size)

    keep = pltpu.make_async_copy(coef, full.at[:, span(o, part)], c_copy)
    keep.start()
    three[...] = jnp.zeros_like(three)
    vir[...] = jnp.zeros_like(vir)
    pl.semaphore_wait(barrier, 3 + nq)

    def relay(chain, src, dst, up, down, across, recv, act):
        pl.when(jnp.logical_and(chain <= z, z < nz - 1))(lambda: act(remote(src, dst, up, recv, (above, s))))
        pl.when(jnp.logical_and(chain >= z, z > 0))(lambda: act(remote(src, dst, down, recv, (below, s))))
        act(remote(src, dst, across, recv, (side, s)))

    def start(copy):
        copy.start()

    def sent(copy):
        copy.wait_send()

    def coef_slot(block):
        return full.at[c, span(block, part)]

    def coef_relay(chain, src, act):
        block = 2 * chain + low
        relay(chain, src, coef_slot(block), c_up.at[chain], c_down.at[chain], c_side.at[chain], c_recv.at[block], act)

    def coef_across(block):
        return remote(coef_slot(block), coef_slot(block), cp_send.at[block], cp_recv.at[block], partner)

    def coef_arrived(block):
        remote(coef_slot(block), coef_slot(block), c_side.at[0], c_recv.at[block], (side, s)).wait_recv()
        coef_across(block).start()

    coef_relay(z, coef.at[c], start)

    @pl.loop(1, nz)
    def _(k):
        chain = nearest_first(z, k, nz)
        block = 2 * chain + low
        remote(coef_slot(block), coef_slot(block), c_side.at[0], c_recv.at[block], (side, s)).wait_recv()
        coef_relay(chain, coef_slot(block), start)
        coef_across(block).start()
        coef_arrived(2 * nearest_first(z, k - 1, nz) + 1 - low)

    coef_arrived(2 * nearest_first(z, nz - 1, nz) + 1 - low)

    @pl.loop(1, n)
    def _(d):
        block = (o + d) % n
        other = full.at[1 - c, span(block, part)]
        remote(other, other, cp_send.at[block], cp_recv.at[block], partner).wait_recv()

    keep.wait()
    fetch.wait()

    def transform(block, rows):
        contract = (((1,), (1,)), ((), ()))
        return sum(
            lax.dot_general(
                full[h, rows, :], ints[block, :, h * cut : (h + 1) * cut], contract, preferred_element_type=F32
            )
            for h in range(2)
        ).astype(jnp.bfloat16)

    order = list(range(1, nq)) + [0]

    def chunk(there, core, group):
        return own.at[there, core, group]

    def to_partner(r):
        ref = chunk(q, c, (q + r) % nq)
        return remote(ref, ref, pr_send.at[r], pr_recv.at[r], partner)

    def to_chip(d, r):
        ref = chunk(q, c, (q + r) % nq)
        return remote(ref, ref, own_send.at[d, r], own_recv.at[d, r], (o, 2 * ((q + d) % nq) + c))

    def onward(d, r, core):
        there = (q + nq - d) % nq
        ref = chunk(there, core, (there + r) % nq)
        return remote(ref, ref, fw_send.at[d, r], fw_recv.at[d, r], partner)

    def from_chip(d, r):
        there = (q + nq - d) % nq
        ref = chunk(there, c, (there + r) % nq)
        remote(ref, ref, own_send.at[d, r], own_recv.at[d, r], partner).wait_recv()
        onward(d, r, c).start()

    for r in order:
        group = (q + r) % nq
        own[q, c, group] = transform(o, span(group, 2 * width))
        for d in range(1, nq):
            to_chip(d, r).start()
        to_partner(r).start()

    def give(block, core):
        return remote(
            gift.at[block], held.at[q, core, span(block, width)], g_send.at[block], g_recv.at[block], partner
        )

    @pl.loop(1, n)
    def _(d):
        block = (o + d) % n
        gift[block] = transform(block, span(2 * q + 1 - c, width))
        give(block, c).start()
        held[q, c, span(block, width), :] = transform(block, span(s, width))

    def held_slot(d, block):
        return held.at[(q + nq - d) % nq, :, span(block, width)]

    def own_slot(d):
        return own.at[(q + nq - d) % nq, :, q, span(c, width)]

    def held_relay(d, chain, src, act):
        block = 2 * chain + low
        relay(
            chain, src, held_slot(d, block), h_up.at[d, chain], h_down.at[d, chain], h_side.at[d, chain],
            h_recv.at[d, block], act,
        )

    def arrived(block):
        for d in range(1, nq):
            ref = held_slot(d, block)
            remote(ref, ref, h_side.at[d, 0], h_recv.at[d, block], (side, s)).wait_recv()

    for d in range(1, nq):
        from_chip(d, d)
    for d in range(1, nq):
        onward(d, d, 1 - c).wait_recv()
        held_relay(d, z, own_slot(d), start)
    rest = [(d, r) for d in range(1, nq) for r in order if r != d]
    for d, r in rest:
        from_chip(d, r)
    for r in order:
        ref = chunk(q, 1 - c, (q + r) % nq)
        remote(ref, ref, pr_send.at[r], pr_recv.at[r], partner).wait_recv()

    @pl.loop(1, n)
    def _(d):
        give((o + d) % n, 1 - c).wait_recv()

    for d, r in rest:
        onward(d, r, 1 - c).wait_recv()
    mine = pltpu.make_async_copy(
        own.at[:, :, q, span(c, width)], held.at[:, :, span(o, width)], o_copy
    )
    mine.start()
    mine.wait()

    def absorb(block):
        rows = span(block, width)
        coulomb = sum(
            lax.dot_general(
                held[t // 2, t % 2, rows, :], own[t // 2, t % 2].reshape(virtuals, -1),
                (((1,), (1,)), ((), ())), preferred_element_type=F32,
            )
            for t in range(2 * nq)
        )
        denominator = occ_e[o] + occ_e[block] - col_e[...] - row_e[...]
        amps[rows, :] = (coulomb / denominator).astype(jnp.bfloat16)

    def pair(chain):
        absorb(2 * chain + low)
        arrived(2 * chain + 1 - low)
        absorb(2 * chain + 1 - low)
        rows = span(chain, 2 * width)
        contract = (((0,), (0,)), ((), ()))

        @pl.loop(0, virtuals // 256)
        def _(t):
            cols = span(t, 256)
            vir[cols, :] += lax.dot_general(amps[rows, cols], amps[rows, :], contract, preferred_element_type=F32)

        @pl.loop(0, 2 * nq)
        def _(t):
            three[t // 2, t % 2] += lax.dot_general(
                held[t // 2, t % 2, rows, :], amps[rows, :], contract, preferred_element_type=F32
            )

    @pl.loop(1, nz)
    def _(k):
        chain = nearest_first(z, k, nz)
        arrived(2 * chain + low)
        for d in range(1, nq):
            held_relay(d, chain, held_slot(d, 2 * chain + low), start)
        pair(nearest_first(z, k - 1, nz))

    pair(nearest_first(z, nz - 1, nz))

    @pl.loop(0, nz)
    def _(chain):
        coef_relay(chain, coef_slot(2 * chain + low), sent)
        for d in range(1, nq):
            held_relay(d, chain, held_slot(d, 2 * chain + low), sent)

    @pl.loop(1, n)
    def _(d):
        block = (o + d) % n
        coef_across(block).wait_send()
        give(block, c).wait_send()

    for r in order:
        to_partner(r).wait_send()
        for d in range(1, nq):
            to_chip(d, r).wait_send()
            onward(d, r, c).wait_send()


def reduce_kernel(
    n, nq, three, vir, three_out, far_out, vir_out,
    t_pair, t_out, t_far, v_pair, v_sum, v_side, v_line, v_chain, v_col, v_far,
    pair_send, pair_recv, t_send, t_recv, vp_send, vp_recv, x_send, x_recv, z_send, z_recv, y_send, y_recv,
):
    o = lax.axis_index("occ")
    s = lax.axis_index("aux")
    q, c = s // 2, s % 2
    z, low = o // 2, o % 2
    nz = n // 2
    partner = (o, 2 * q + 1 - c)
    side = (2 * z + 1 - low, s)

    barrier = pltpu.get_barrier_semaphore()
    pl.semaphore_signal(barrier, inc=1, device_id=partner, device_id_type=MESH)
    pl.semaphore_signal(barrier, inc=1, device_id=side, device_id_type=MESH)
    for d in range(1, nq):
        pl.semaphore_signal(barrier, inc=1, device_id=(o, 2 * ((q + d) % nq) + c), device_id_type=MESH)
    for d in range(1, nz):
        pl.semaphore_signal(barrier, inc=1, device_id=(2 * ((z + d) % nz) + low, s), device_id_type=MESH)
    pl.semaphore_wait(barrier, nq + nz)

    v_swap = remote(vir.at[:, :, 1 - c], v_pair, vp_send, vp_recv, partner)
    v_swap.start()

    def swap(d):
        there = (q + d) % nq
        return remote(three.at[there, 1 - c], t_pair.at[d], pair_send.at[d], pair_recv.at[d], partner)

    def spread(d):
        return remote(t_out.at[d], t_far.at[d], t_send.at[d], t_recv.at[d], (o, 2 * ((q + d) % nq) + c))

    order = list(range(1, nq)) + [0]
    for d in order:
        swap(d).start()
    v_swap.wait()
    v_sum[...] = (vir[:, :, c] + v_pair[...]).reshape(v_sum.shape)
    x_swap = remote(v_sum.at[:, 1 - low], v_side, x_send, x_recv, side)
    x_swap.start()
    for d in order[:-1]:
        swap(d).wait()
        t_out[d] = three[(q + d) % nq, c] + t_pair[d]
        spread(d).start()
    swap(0).wait()
    three_out[...] = three[q, c] + t_pair[0]

    x_swap.wait()
    v_line[...] = v_sum[:, low] + v_side[...]

    def along(d):
        there = (z + d) % nz
        return remote(v_line.at[there], v_chain.at[d], z_send.at[d], z_recv.at[d], (2 * there + low, s))

    for d in range(1, nz):
        along(d).start()
    v_col[...] = v_line[z]
    for d in range(1, nz):
        along(d).wait()
        v_col[...] += v_chain[d]

    def between(d):
        there = (q + d) % nq
        return remote(v_col.at[there], v_far.at[d], y_send.at[d], y_recv.at[d], (o, 2 * there + c))

    for d in range(1, nq):
        between(d).start()
    for d in order[:-1]:
        spread(d).wait()
        far_out[...] = t_far[d] if d == 1 else far_out[...] + t_far[d]
    rows = v_col[q]
    for d in range(1, nq):
        between(d).wait()
        rows += v_far[d]
    vir_out[...] = rows


def per_device(half_integrals, vir_coef, occ_energy, vir_energy):
    n, aux = lax.axis_size("occ"), lax.axis_size("aux")
    nz, nq = n // 2, aux // 2
    _, tile, basis = half_integrals.shape
    part = vir_coef.shape[1]
    virtuals = part * n
    width, rows = virtuals // aux, virtuals // (n * aux)
    coef = vir_coef.reshape(2, basis // 2, part).transpose(0, 2, 1)
    row_e = vir_energy[None, :]
    col_e = lax.dynamic_slice_in_dim(vir_energy, lax.axis_index("aux") * width, width, 0)[:, None]
    vmem = pl.BlockSpec(memory_space=pltpu.VMEM)
    dma = pltpu.SemaphoreType.DMA
    half = jnp.bfloat16
    three, vir = pl.pallas_call(
        functools.partial(amplitude_kernel, n, nq),
        out_shape=(
            jax.ShapeDtypeStruct((nq, 2, tile, virtuals), F32),
            jax.ShapeDtypeStruct((virtuals, virtuals), F32),
        ),
        in_specs=[pl.BlockSpec(memory_space=pltpu.SMEM), pl.BlockSpec(memory_space=pl.ANY), vmem, vmem, vmem],
        out_specs=(vmem, vmem),
        scratch_shapes=[
            pltpu.VMEM(half_integrals.shape, half),
            pltpu.VMEM((2, virtuals, basis // 2), half),
            pltpu.VMEM((nq, 2, nq, 2 * width, tile), half),
            pltpu.VMEM((nq, 2, n * width, tile), half),
            pltpu.VMEM((n, width, tile), half),
            pltpu.VMEM((n * width, virtuals), half),
            dma, dma, dma, dma((n,)), dma((nz,)), dma((nz,)), dma((nz,)), dma((n,)), dma((n,)),
            dma((nq, nq)), dma((nq, nq)), dma((nq, nq)), dma((nq, nq)), dma((nq,)), dma((nq,)), dma((n,)), dma((n,)),
            dma((nq, n)), dma((nq, nz)), dma((nq, nz)), dma((nq, nz)),
        ],
        compiler_params=pltpu.CompilerParams(
            collective_id=0, has_side_effects=True, vmem_limit_bytes=LIMIT
        ),
        name="amplitude",
    )(occ_energy, half_integrals, coef, row_e, col_e)

    def room(*shape):
        return pltpu.VMEM(shape, F32)

    near, far, vir_rows = pl.pallas_call(
        functools.partial(reduce_kernel, n, nq),
        out_shape=(
            jax.ShapeDtypeStruct((tile, virtuals), F32),
            jax.ShapeDtypeStruct((tile, virtuals), F32),
            jax.ShapeDtypeStruct((rows, virtuals), F32),
        ),
        in_specs=[vmem, vmem],
        out_specs=(vmem, vmem, vmem),
        scratch_shapes=[
            room(nq, tile, virtuals), room(nq, tile, virtuals), room(nq, tile, virtuals),
            room(n, nq, rows, virtuals), room(nz, 2, nq, rows, virtuals),
            room(nz, nq, rows, virtuals), room(nz, nq, rows, virtuals), room(nz, nq, rows, virtuals),
            room(nq, rows, virtuals), room(nq, rows, virtuals),
            dma((nq,)), dma((nq,)), dma((nq,)), dma((nq,)), dma, dma, dma, dma,
            dma((nz,)), dma((nz,)), dma((nq,)), dma((nq,)),
        ],
        compiler_params=pltpu.CompilerParams(
            collective_id=1, has_side_effects=True, vmem_limit_bytes=LIMIT
        ),
        name="reduce",
    )(
        three,
        vir.reshape(n, nq, 2, rows, virtuals),
    )
    return (near + far)[:, None, :], vir_rows / (n * virtuals)


def solution(mesh):
    return jax.shard_map(
        per_device,
        mesh=mesh,
        in_specs=(P(None, "aux", None), P(None, "occ"), P(), P()),
        out_specs=(P("aux", "occ", None), P(("occ", "aux"), None)),
        check_vma=False,
    )
```

time: 151 us -> 112 us (0.74)
  blocking collectives: 19.2 us -> 0 us
  waiting for transfers between devices: 17.3 us -> 0 us
  between operations: 14.1 us -> 0.66 us
  Pallas kernels: 90.3 us -> 103 us
  matrix products: 3.6 us -> 0 us
  other arithmetic: 0 us -> 2.13 us
    all_to_all x1 -> x0, blocking collectives: 19.2 us -> none  [per_device(): lax.all_to_all(partial_block, 'occ', split_axis=0, concat_axis=1, tiled=T...]
    all_gather x1 -> x0, waiting for transfers between devices: 17.2 us -> none  [per_device(): own = lax.all_gather(local_block, 'aux', axis=2, tiled=True)[0]]
    pallas_call x2, Pallas kernels: 90.3 us -> 103 us  [the longest x1 60.3 us: per_device(): pl.pallas_call(functools.partial(amplitude_kernel, n, nq), out_shape=(jax...]
    dot_general x1 -> x0, matrix products: 3.6 us -> none  [per_device(): jnp.einsum('ipm,ma->iap', half_integrals, vir_coef, preferred_element_typ...]
    unnamed x6 -> x3, local copies, waits for them, and re-layouts: 5.22 us -> 1.69 us
    reshape x0 -> x1, local copies, waits for them, and re-layouts: none -> 1.62 us  [per_device(): coef = vir_coef.reshape(2, basis // 2, part).transpose(0, 2, 1)]
  transfers between devices with their start and end apart: 1 -> 0, of which waited for: 1 -> 0; matrix products, arithmetic and copies ran while one was open for 1% -> 0% of each run, Pallas kernels for 0% -> 0%
where the time goes in v2:
time: 112 us; the launch traced here: 111 us
  Pallas kernels  103 us (92%)
  local copies, waits for them, and re-layouts  6.12 us (5%)
  other arithmetic  2.13 us (2%)
    pallas_call x1, Pallas kernels, per_device(): pl.pallas_call(functools.partial(amplitude_kernel, n, nq), out_shape=(jax...  60.3 us
    pallas_call x1, Pallas kernels, per_device(): pl.pallas_call(functools.partial(reduce_kernel, n, nq), out_shape=(jax.Sh...  42.2 us

profile of v2, /device:TPU:0, one launch (start us, length us, event | category | flops | bytes accessed | tf_op | source)
XLA Modules:
  0.0 111.5 jit_solution(11212774145403878801)
XLA Ops:
  0.6 0.8 dynamic_slice.3
  1.4 1.3 %broadcast_in_dim.9.row_e = f32[1,768]{1,0:T(1,128)} reshape(f32[768]{0:T(1024)} %param.7) | data formatting | bytes 6144 | tf_op jit(solution)/shard_map/broadcast_in_dim | solution.py:351
  2.7 0.8 copy.8.col_e
  3.4 1.6 %copy.12 = bf16[12,2,8,512]{3,2,0,1:T(8,128)(2,1)} copy(bf16[12,2,8,512]{3,2,1,0:T(8,128)(2,1)} %bitcast.13) | data formatting | bytes 393216 | tf_op jit(solution)/shard_map/reshape | solution.py:350
  5.1 60.3 %amplitude.1 = (f32[2,2,256,768]{3,2,1,0:T(8,128)}, f32[768,768]{1,0:T(8,128)}) custom-call(f32[8]{0:T(128)} %occ_e.1, bf16[8,256,1024]{2,1,0:T(8,128)(2,1)} %half.1, bf16[2,96,512]{2,1,0:T(8,128)(2,1)} %bitcast.12, f32[1,768]{1,0:T(1,128)} %broadcast_in_dim.9.row_e, f32[192,1]{1,0:T(8,128)} %copy.8.col_e), custom_call_target="tpu_custom_call" | custom-call | tf_op jit(solution)/shard_map/amplitude/pallas_call | solution.py:356
  65.4 42.2 %reduce.1 = (f32[256,768]{1,0:T(8,128)}, f32[256,768]{1,0:T(8,128)}, f32[24,768]{1,0:T(8,128)}) custom-call(f32[2,2,256,768]{3,2,1,0:T(8,128)} %get-tuple-element.7.three, f32[8,2,2,24,768]{4,3,2,1,0:T(8,128)} %bitcast.11), custom_call_target="tpu_custom_call" | custom-call | tf_op jit(solution)/shard_map/reduce/pallas_call | solution.py:384
  107.6 0.0 copy-start
  107.6 1.5 %add_bitcast_fusion = f32[256,1,768]{2,0,1:T(8,128)S(1)} fusion(f32[256,768]{1,0:T(8,128)} %get-tuple-element.9, f32[256,768]{1,0:T(8,128)} %get-tuple-element.10), kind=kLoop, calls=%fused_computation | loop fusion | flops 196608 | bytes 2359296 | tf_op jit(solution)/shard_map/broadcast_in_dim | solution.py:409
  109.1 1.7 %copy.9 = f32[256,1,768]{2,1,0:T(1,128)} copy(f32[256,1,768]{2,0,1:T(8,128)S(1)} %add_bitcast_fusion) | data formatting | bytes 1572864
  110.8 0.0 copy-done
  110.8 0.6 broadcast_multiply_fusion
Async XLA Ops:
  107.6 3.2 %copy-start = (f32[24,768]{1,0:T(8,128)S(1)}, f32[24,768]{1,0:T(8,128)}, u32[]{:S(2)}) copy-start(f32[24,768]{1,0:T(8,128)} %get-tuple-element.11) | copy-start | bytes 221188

commit v3 on v2

v3 whole, which is shorter than its diff:
```python
import functools

import jax
import jax.numpy as jnp
from jax import lax
from jax.experimental import pallas as pl
from jax.experimental.pallas import tpu as pltpu
from jax.sharding import PartitionSpec as P

MESH = pl.DeviceIdType.MESH
F32 = jnp.float32
LIMIT = 56 * 1024 * 1024


def remote(src, dst, send, recv, target):
    return pltpu.make_async_remote_copy(
        src_ref=src, dst_ref=dst, send_sem=send, recv_sem=recv, device_id=target, device_id_type=MESH
    )


def nearest_first(z, k, count):
    near = jnp.minimum(z, count - 1 - z)
    step = (k + 1) // 2
    both = z + step * (2 * (k % 2) - 1)
    low = z < count - 1 - z
    return jnp.where(k <= 2 * near, both, jnp.where(low, k, count - 1 - k))


def greet(n, nq):
    o = lax.axis_index("occ")
    s = lax.axis_index("aux")
    q, c = s // 2, s % 2
    z, low = o // 2, o % 2
    nz = n // 2
    barrier = pltpu.get_barrier_semaphore()
    peers = [(2 * z + 1 - low, s), (o, 2 * q + 1 - c)]
    peers += [(o, 2 * ((q + d) % nq) + c) for d in range(1, nq)]
    peers += [(2 * ((z + d) % nz) + low, s) for d in range(1, nz)]
    for peer in peers:
        pl.semaphore_signal(barrier, inc=1, device_id=peer, device_id_type=MESH)
    return lambda: pl.semaphore_wait(barrier, len(peers))


def make_densities(
    n, nq, occ_e, half, coef, vir_e, three, vir,
    ints, full, own, held, gift, amps,
    i_sem, c_copy, o_copy, c_recv, c_up, c_down, c_side, cp_send, cp_recv,
    own_send, own_recv, fw_send, fw_recv, pr_send, pr_recv, g_send, g_recv,
    h_recv, h_up, h_down, h_side,
    vir_done=lambda: None,
):
    o = lax.axis_index("occ")
    s = lax.axis_index("aux")
    q, c = s // 2, s % 2
    z, low = o // 2, o % 2
    nz = n // 2
    width = amps.shape[0] // n
    part = coef.shape[0]
    cut = coef.shape[1] // 2
    virtuals = amps.shape[1]
    above, below, side = o + 2, o - 2, 2 * z + 1 - low
    partner = (o, 2 * q + 1 - c)
    entered = greet(n, nq)

    fetch = pltpu.make_async_copy(half, ints, i_sem)
    fetch.start()

    def span(index, size):
        return pl.ds(pl.multiple_of(index * size, size), size)

    def keep(h):
        return pltpu.make_async_copy(coef.at[:, h * cut : (h + 1) * cut], full.at[h, span(o, part)], c_copy.at[h])

    keep(0).start()
    keep(1).start()
    entered()

    def relay(chain, src, dst, up, down, across, recv, act):
        pl.when(jnp.logical_and(chain <= z, z < nz - 1))(lambda: act(remote(src, dst, up, recv, (above, s))))
        pl.when(jnp.logical_and(chain >= z, z > 0))(lambda: act(remote(src, dst, down, recv, (below, s))))
        act(remote(src, dst, across, recv, (side, s)))

    def start(copy):
        copy.start()

    def sent(copy):
        copy.wait_send()

    def coef_slot(block):
        return full.at[c, span(block, part)]

    def coef_relay(chain, src, act):
        block = 2 * chain + low
        relay(chain, src, coef_slot(block), c_up.at[chain], c_down.at[chain], c_side.at[chain], c_recv.at[block], act)

    def coef_across(block):
        return remote(coef_slot(block), coef_slot(block), cp_send.at[block], cp_recv.at[block], partner)

    def coef_arrived(block):
        remote(coef_slot(block), coef_slot(block), c_side.at[0], c_recv.at[block], (side, s)).wait_recv()
        coef_across(block).start()

    coef_relay(z, coef.at[:, span(c, cut)], start)
    three[...] = jnp.zeros_like(three)
    vir[...] = jnp.zeros_like(vir)
    row_e = vir_e[...].reshape(1, virtuals)
    here = lax.broadcasted_iota(jnp.int32, (width, virtuals), 0) + s * width
    there = lax.broadcasted_iota(jnp.int32, (width, virtuals), 1)
    col_e = jnp.sum(jnp.where(here == there, row_e, 0.0), axis=1, keepdims=True)

    @pl.loop(1, nz)
    def _(k):
        chain = nearest_first(z, k, nz)
        block = 2 * chain + low
        remote(coef_slot(block), coef_slot(block), c_side.at[0], c_recv.at[block], (side, s)).wait_recv()
        coef_relay(chain, coef_slot(block), start)
        coef_across(block).start()
        coef_arrived(2 * nearest_first(z, k - 1, nz) + 1 - low)

    coef_arrived(2 * nearest_first(z, nz - 1, nz) + 1 - low)

    @pl.loop(1, n)
    def _(d):
        block = (o + d) % n
        other = full.at[1 - c, span(block, part)]
        remote(other, other, cp_send.at[block], cp_recv.at[block], partner).wait_recv()

    keep(0).wait()
    keep(1).wait()
    fetch.wait()

    def transform(block, rows):
        contract = (((1,), (1,)), ((), ()))
        return sum(
            lax.dot_general(
                full[h, rows, :], ints[block, :, h * cut : (h + 1) * cut], contract, preferred_element_type=F32
            )
            for h in range(2)
        ).astype(jnp.bfloat16)

    order = list(range(1, nq)) + [0]

    def chunk(there, core, group):
        return own.at[there, core, group]

    def to_partner(r):
        ref = chunk(q, c, (q + r) % nq)
        return remote(ref, ref, pr_send.at[r], pr_recv.at[r], partner)

    def to_chip(d, r):
        ref = chunk(q, c, (q + r) % nq)
        return remote(ref, ref, own_send.at[d, r], own_recv.at[d, r], (o, 2 * ((q + d) % nq) + c))

    def onward(d, r, core):
        there = (q + nq - d) % nq
        ref = chunk(there, core, (there + r) % nq)
        return remote(ref, ref, fw_send.at[d, r], fw_recv.at[d, r], partner)

    def from_chip(d, r):
        there = (q + nq - d) % nq
        ref = chunk(there, c, (there + r) % nq)
        remote(ref, ref, own_send.at[d, r], own_recv.at[d, r], partner).wait_recv()
        onward(d, r, c).start()

    for r in order:
        group = (q + r) % nq
        own[q, c, group] = transform(o, span(group, 2 * width))
        for d in range(1, nq):
            to_chip(d, r).start()
        to_partner(r).start()

    def give(block, core):
        return remote(
            gift.at[block], held.at[q, core, span(block, width)], g_send.at[block], g_recv.at[block], partner
        )

    @pl.loop(1, n)
    def _(d):
        block = (o + d) % n
        gift[block] = transform(block, span(2 * q + 1 - c, width))
        give(block, c).start()
        held[q, c, span(block, width), :] = transform(block, span(s, width))

    def held_slot(d, block):
        return held.at[(q + nq - d) % nq, :, span(block, width)]

    def own_slot(d):
        return own.at[(q + nq - d) % nq, :, q, span(c, width)]

    def held_relay(d, chain, src, act):
        block = 2 * chain + low
        relay(
            chain, src, held_slot(d, block), h_up.at[d, chain], h_down.at[d, chain], h_side.at[d, chain],
            h_recv.at[d, block], act,
        )

    def arrived(block):
        for d in range(1, nq):
            ref = held_slot(d, block)
            remote(ref, ref, h_side.at[d, 0], h_recv.at[d, block], (side, s)).wait_recv()

    for d in range(1, nq):
        from_chip(d, d)
    for d in range(1, nq):
        onward(d, d, 1 - c).wait_recv()
        held_relay(d, z, own_slot(d), start)
    rest = [(d, r) for d in range(1, nq) for r in order if r != d]
    for d, r in rest:
        from_chip(d, r)
    for r in order:
        ref = chunk(q, 1 - c, (q + r) % nq)
        remote(ref, ref, pr_send.at[r], pr_recv.at[r], partner).wait_recv()

    @pl.loop(1, n)
    def _(d):
        give((o + d) % n, 1 - c).wait_recv()

    for d, r in rest:
        onward(d, r, 1 - c).wait_recv()
    mine = pltpu.make_async_copy(
        own.at[:, :, q, span(c, width)], held.at[:, :, span(o, width)], o_copy
    )
    mine.start()
    mine.wait()

    def absorb(block):
        rows = span(block, width)
        coulomb = sum(
            lax.dot_general(
                held[t // 2, t % 2, rows, :], own[t // 2, t % 2].reshape(virtuals, -1),
                (((1,), (1,)), ((), ())), preferred_element_type=F32,
            )
            for t in range(2 * nq)
        )
        denominator = occ_e[o] + occ_e[block] - col_e - row_e
        amps[rows, :] = (coulomb / denominator).astype(jnp.bfloat16)

    contract = (((0,), (0,)), ((), ()))
    piece = virtuals // 2 if len(vir.shape) > 2 else 256

    def add_vir(chain):
        rows = span(chain, 2 * width)

        @pl.loop(0, virtuals // piece)
        def _(t):
            new = lax.dot_general(
                amps[rows, span(t, piece)], amps[rows, :], contract, preferred_element_type=F32
            )
            where = span(t, vir.shape[0] * piece // virtuals)
            vir[where] += new.reshape((-1,) + vir.shape[1:])

    def add_three(chain):
        rows = span(chain, 2 * width)

        @pl.loop(0, 2 * nq)
        def _(t):
            three[t // 2, t % 2] += lax.dot_general(
                held[t // 2, t % 2, rows, :], amps[rows, :], contract, preferred_element_type=F32
            )

    def both(chain):
        absorb(2 * chain + low)
        arrived(2 * chain + 1 - low)
        absorb(2 * chain + 1 - low)

    @pl.loop(1, nz)
    def _(k):
        chain = nearest_first(z, k, nz)
        arrived(2 * chain + low)
        for d in range(1, nq):
            held_relay(d, chain, held_slot(d, 2 * chain + low), start)
        before = nearest_first(z, k - 1, nz)
        both(before)
        add_vir(before)
        add_three(before)

    last = nearest_first(z, nz - 1, nz)
    both(last)
    add_vir(last)
    vir_done()
    add_three(last)

    def finish():
        @pl.loop(0, nz)
        def _(chain):
            coef_relay(chain, coef_slot(2 * chain + low), sent)
            for d in range(1, nq):
                held_relay(d, chain, held_slot(d, 2 * chain + low), sent)

        @pl.loop(1, n)
        def _(d):
            block = (o + d) % n
            coef_across(block).wait_send()
            give(block, c).wait_send()

        for r in order:
            to_partner(r).wait_send()
            for d in range(1, nq):
                to_chip(d, r).wait_send()
                onward(d, r, c).wait_send()

    return finish


def reduction(
    n, nq, three, vir, near_out, far_out, vir_out,
    t_pair, t_out, t_far, v_pair, v_sum, v_side, v_line, v_chain, v_col, v_far,
    pair_send, pair_recv, t_send, t_recv, vp_send, vp_recv, x_send, x_recv, z_send, z_recv, y_send, y_recv,
):
    o = lax.axis_index("occ")
    s = lax.axis_index("aux")
    q, c = s // 2, s % 2
    z, low = o // 2, o % 2
    nz = n // 2
    chunks, chunk = v_pair.shape[0], v_pair.shape[-1]
    partner = (o, 2 * q + 1 - c)
    side = (2 * z + 1 - low, s)

    def cols(k):
        return pl.ds(k * chunk, chunk)

    def v_swap(k):
        return remote(vir.at[:, :, 1 - c, :, cols(k)], v_pair.at[k], vp_send.at[k], vp_recv.at[k], partner)

    def x_swap(k):
        return remote(v_sum.at[k, :, 1 - low], v_side.at[k], x_send.at[k], x_recv.at[k], side)

    def along(k, d):
        there = (z + d) % nz
        return remote(
            v_line.at[k, there], v_chain.at[k, d], z_send.at[k, d], z_recv.at[k, d], (2 * there + low, s)
        )

    def between(k, d):
        there = (q + d) % nq
        return remote(v_col.at[k, there], v_far.at[k, d], y_send.at[k, d], y_recv.at[k, d], (o, 2 * there + c))

    def swap(d):
        return remote(three.at[(q + d) % nq, 1 - c], t_pair.at[d], pair_send.at[d], pair_recv.at[d], partner)

    def spread(d):
        return remote(t_out.at[d], t_far.at[d], t_send.at[d], t_recv.at[d], (o, 2 * ((q + d) % nq) + c))

    order = list(range(1, nq)) + [0]

    def open_vir():
        for k in range(chunks):
            v_swap(k).start()

    def close():
        for d in order:
            swap(d).start()
        for k in range(chunks):
            v_swap(k).wait()
            v_sum[k] = (vir[:, :, c, :, cols(k)] + v_pair[k]).reshape(v_sum.shape[1:])
            x_swap(k).start()
        for d in order[:-1]:
            swap(d).wait()
            t_out[d] = three[(q + d) % nq, c] + t_pair[d]
            spread(d).start()
        for k in range(chunks):
            x_swap(k).wait()
            v_line[k] = v_sum[k, :, low] + v_side[k]
            for d in range(1, nz):
                along(k, d).start()
            if k == 0:
                swap(0).wait()
                near_out[...] = three[q, c] + t_pair[0]
        for k in range(chunks):
            held = v_line[k, z]
            for d in range(1, nz):
                along(k, d).wait()
                held += v_chain[k, d]
            v_col[k] = held
            for d in range(1, nq):
                between(k, d).start()
        for d in order[:-1]:
            spread(d).wait()
            far_out[...] = t_far[d] if d == 1 else far_out[...] + t_far[d]
        for k in range(chunks):
            rows = v_col[k, q]
            for d in range(1, nq):
                between(k, d).wait()
                rows += v_far[k, d]
            vir_out[:, cols(k)] = rows

    return open_vir, close


def amplitude_kernel(n, nq, *refs):
    make_densities(n, nq, *refs)()


def reduce_kernel(n, nq, *refs):
    greet(n, nq)()
    open_vir, close = reduction(n, nq, *refs)
    open_vir()
    close()


def whole_kernel(n, nq, inputs, outputs, count, *refs):
    operands, results, scratch = refs[:inputs], refs[inputs : inputs + outputs], refs[inputs + outputs :]
    three, vir, rest = scratch[0], scratch[1], scratch[2:]
    open_vir, close = reduction(n, nq, three, vir, *results, *rest[count:])
    finish = make_densities(n, nq, *operands, three, vir, *rest[:count], vir_done=open_vir)
    close()
    finish()


def per_device(half_integrals, vir_coef, occ_energy, vir_energy):
    n, aux = lax.axis_size("occ"), lax.axis_size("aux")
    nz, nq = n // 2, aux // 2
    _, tile, basis = half_integrals.shape
    part = vir_coef.shape[1]
    virtuals = part * n
    width, rows = virtuals // aux, virtuals // (n * aux)
    vmem = pl.BlockSpec(memory_space=pltpu.VMEM)
    dma = pltpu.SemaphoreType.DMA
    half = jnp.bfloat16
    chunks = virtuals // 256

    def room(*shape):
        return pltpu.VMEM(shape, F32)

    def result(*shape):
        return jax.ShapeDtypeStruct(shape, F32)

    def call(kernel, name, number, in_specs, out_shape, scratch, operands):
        return pl.pallas_call(
            kernel,
            out_shape=out_shape,
            in_specs=in_specs,
            out_specs=(vmem,) * len(out_shape),
            scratch_shapes=scratch,
            compiler_params=pltpu.CompilerParams(
                collective_id=number, has_side_effects=True, vmem_limit_bytes=LIMIT
            ),
            name=name,
        )(*operands)

    operands = (occ_energy, half_integrals, vir_coef.T, vir_energy)
    specs = [pl.BlockSpec(memory_space=pltpu.SMEM), pl.BlockSpec(memory_space=pl.ANY), vmem, vmem]
    make_scratch = [
        pltpu.VMEM(half_integrals.shape, half),
        pltpu.VMEM((2, virtuals, basis // 2), half),
        pltpu.VMEM((nq, 2, nq, 2 * width, tile), half),
        pltpu.VMEM((nq, 2, n * width, tile), half),
        pltpu.VMEM((n, width, tile), half),
        pltpu.VMEM((n * width, virtuals), half),
        dma, dma((2,)), dma, dma((n,)), dma((nz,)), dma((nz,)), dma((nz,)), dma((n,)), dma((n,)),
        dma((nq, nq)), dma((nq, nq)), dma((nq, nq)), dma((nq, nq)), dma((nq,)), dma((nq,)), dma((n,)), dma((n,)),
        dma((nq, n)), dma((nq, nz)), dma((nq, nz)), dma((nq, nz)),
    ]
    reduce_scratch = [
        room(nq, tile, virtuals), room(nq, tile, virtuals), room(nq, tile, virtuals),
        room(chunks, n, nq, rows, 256), room(chunks, nz, 2, nq, rows, 256),
        room(chunks, nz, nq, rows, 256), room(chunks, nz, nq, rows, 256), room(chunks, nz, nq, rows, 256),
        room(chunks, nq, rows, 256), room(chunks, nq, rows, 256),
        dma((nq,)), dma((nq,)), dma((nq,)), dma((nq,)), dma((chunks,)), dma((chunks,)), dma((chunks,)), dma((chunks,)),
        dma((chunks, nz)), dma((chunks, nz)), dma((chunks, nq)), dma((chunks, nq)),
    ]
    sums = (nq, 2, tile, virtuals)
    groups = (n, nq, 2, rows, virtuals)
    finals = (result(tile, virtuals), result(tile, virtuals), result(rows, virtuals))
    if rows % 8 == 0:
        kernel = functools.partial(whole_kernel, n, nq, len(specs), len(finals), len(make_scratch))
        scratch = [room(*sums), room(*groups)] + make_scratch + reduce_scratch
        near, far, vir_rows = call(kernel, "densities", 0, specs, finals, scratch, operands)
    else:
        kernel = functools.partial(amplitude_kernel, n, nq)
        partials = (result(*sums), result(virtuals, virtuals))
        three, vir = call(kernel, "amplitude", 0, specs, partials, make_scratch, operands)
        kernel = functools.partial(reduce_kernel, n, nq)
        near, far, vir_rows = call(
            kernel, "reduce", 1, [vmem, vmem], finals, reduce_scratch, (three, vir.reshape(groups))
        )
    return (near + far)[:, None, :], vir_rows / (n * virtuals)


def solution(mesh):
    return jax.shard_map(
        per_device,
        mesh=mesh,
        in_specs=(P(None, "aux", None), P(None, "occ"), P(), P()),
        out_specs=(P("aux", "occ", None), P(("occ", "aux"), None)),
        check_vma=False,
    )
```

time: 112 us -> 90 us (0.80)
  Pallas kernels: 103 us -> 84.5 us
  local copies, waits for them, and re-layouts: 6.12 us -> 1.69 us
    pallas_call x2 -> x1, Pallas kernels: 103 us -> 84.5 us  [call(): pl.pallas_call(kernel, out_shape=out_shape, in_specs=in_specs, out_specs=...]
    broadcast_in_dim x2 -> x0, local copies, waits for them, and re-layouts: 2.05 us -> none  [the longest x1 1.27 us: per_device(): row_e = vir_energy[None, :]]
    reshape x1 -> x0, local copies, waits for them, and re-layouts: 1.62 us -> none  [per_device(): coef = vir_coef.reshape(2, basis // 2, part).transpose(0, 2, 1)]
where the time goes in v3:
time: 90 us; the launch traced here: 89.8 us
  Pallas kernels  84.5 us (94%)
  other arithmetic  2.98 us (3%)
  local copies, waits for them, and re-layouts  1.69 us (2%)
    pallas_call x1, Pallas kernels, call(): pl.pallas_call(kernel, out_shape=out_shape, in_specs=in_specs, out_specs=...  84.5 us

profile of v3, /device:TPU:0, one launch (start us, length us, event | category | flops | bytes accessed | tf_op | source)
XLA Modules:
  0.0 89.8 jit_solution(17870615391520145019)
XLA Ops:
  0.6 84.5 %densities.1 = (f32[256,768]{1,0:T(8,128)}, f32[256,768]{1,0:T(8,128)}, f32[24,768]{1,0:T(8,128)}) custom-call(f32[8]{0:T(128)} %refs_0_.1, bf16[8,256,1024]{2,1,0:T(8,128)(2,1)} %refs_1_.1, bf16[96,1024]{1,0:T(8,128)(2,1)} %bitcast.3, f32[768]{0:T(1024)} %refs_3_.1), custom_call_target="tpu_custom_call" | custom-call | tf_op jit(solution)/shard_map/densities/pallas_call | solution.py:429
  85.1 1.5 %add_bitcast_fusion = f32[256,1,768]{2,0,1:T(8,128)S(1)} fusion(f32[256,768]{1,0:T(8,128)} %get-tuple-element.5, f32[256,768]{1,0:T(8,128)} %get-tuple-element.6), kind=kLoop, calls=%fused_computation | loop fusion | flops 196608 | bytes 2359296 | tf_op jit(solution)/shard_map/broadcast_in_dim | solution.py:477
  86.6 1.7 %copy.6 = f32[256,1,768]{2,1,0:T(1,128)} copy(f32[256,1,768]{2,0,1:T(8,128)S(1)} %add_bitcast_fusion) | data formatting | bytes 1572864
  88.3 1.5 %broadcast_multiply_fusion = f32[24,768]{1,0:T(8,128)} fusion(f32[24,768]{1,0:T(8,128)} %get-tuple-element.7), kind=kLoop, calls=%fused_computation.1 | loop fusion | flops 18432 | bytes 147456 | tf_op jit(solution)/shard_map/div | solution.py:477

commit v4 on v3

--- a/solution.py
+++ b/solution.py
@@ -417,7 +417,8 @@
     vmem = pl.BlockSpec(memory_space=pltpu.VMEM)
     dma = pltpu.SemaphoreType.DMA
     half = jnp.bfloat16
-    chunks = virtuals // 256
+    lanes = 128
+    chunks = virtuals // lanes
 
     def room(*shape):
         return pltpu.VMEM(shape, F32)
@@ -453,9 +454,9 @@
     ]
     reduce_scratch = [
         room(nq, tile, virtuals), room(nq, tile, virtuals), room(nq, tile, virtuals),
-        room(chunks, n, nq, rows, 256), room(chunks, nz, 2, nq, rows, 256),
-        room(chunks, nz, nq, rows, 256), room(chunks, nz, nq, rows, 256), room(chunks, nz, nq, rows, 256),
-        room(chunks, nq, rows, 256), room(chunks, nq, rows, 256),
+        room(chunks, n, nq, rows, lanes), room(chunks, nz, 2, nq, rows, lanes),
+        room(chunks, nz, nq, rows, lanes), room(chunks, nz, nq, rows, lanes), room(chunks, nz, nq, rows, lanes),
+        room(chunks, nq, rows, lanes), room(chunks, nq, rows, lanes),
         dma((nq,)), dma((nq,)), dma((nq,)), dma((nq,)), dma((chunks,)), dma((chunks,)), dma((chunks,)), dma((chunks,)),
         dma((chunks, nz)), dma((chunks, nz)), dma((chunks, nq)), dma((chunks, nq)),
     ]

time: 90 us -> 89.4 us (level)
  no operation moved by 1% of the time
where the time goes in v4:
time: 89.4 us; the launch traced here: 89.2 us
  Pallas kernels  83.9 us (94%)
  other arithmetic  2.98 us (3%)
  local copies, waits for them, and re-layouts  1.69 us (2%)
    pallas_call x1, Pallas kernels, call(): pl.pallas_call(kernel, out_shape=out_shape, in_specs=in_specs, out_specs=...  83.9 us

profile of v4, /device:TPU:0, one launch (start us, length us, event | category | flops | bytes accessed | tf_op | source)
XLA Modules:
  0.0 89.2 jit_solution(14951842854237546676)
XLA Ops:
  0.6 83.9 %densities.1 = (f32[256,768]{1,0:T(8,128)}, f32[256,768]{1,0:T(8,128)}, f32[24,768]{1,0:T(8,128)}) custom-call(f32[8]{0:T(128)} %refs_0_.1, bf16[8,256,1024]{2,1,0:T(8,128)(2,1)} %refs_1_.1, bf16[96,1024]{1,0:T(8,128)(2,1)} %bitcast.3, f32[768]{0:T(1024)} %refs_3_.1), custom_call_target="tpu_custom_call" | custom-call | tf_op jit(solution)/shard_map/densities/pallas_call | solution.py:430
  84.5 1.5 %add_bitcast_fusion = f32[256,1,768]{2,0,1:T(8,128)S(1)} fusion(f32[256,768]{1,0:T(8,128)} %get-tuple-element.5, f32[256,768]{1,0:T(8,128)} %get-tuple-element.6), kind=kLoop, calls=%fused_computation | loop fusion | flops 196608 | bytes 2359296 | tf_op jit(solution)/shard_map/broadcast_in_dim | solution.py:478
  86.0 1.7 %copy.6 = f32[256,1,768]{2,1,0:T(1,128)} copy(f32[256,1,768]{2,0,1:T(8,128)S(1)} %add_bitcast_fusion) | data formatting | bytes 1572864
  87.7 1.5 %broadcast_multiply_fusion = f32[24,768]{1,0:T(8,128)} fusion(f32[24,768]{1,0:T(8,128)} %get-tuple-element.7), kind=kLoop, calls=%fused_computation.1 | loop fusion | flops 18432 | bytes 147456 | tf_op jit(solution)/shard_map/div | solution.py:478
